TPU v7x, 32 devices: a whole 2x2x4 slice. The times are simulated.
32 devices in a mesh: win: 2 (over x), wide: 8 (over z, y), narrow: 2 (over core).
Axes of the slice: x: 2, y: 2, z: 4, core: 2. Of those that a mesh axis runs over, the one named last changes fastest.
Arguments:
- window_data: float32 [384, 128, 256], P(('win', 'wide'), 'narrow'), parts along dimension 0, may hold values from -6 to 6
- factor_one: float32 [256, 48], P(('win', 'narrow')), parts along dimension 0, may hold values from -0.5 to 0.5
- factor_two: float32 [512, 48], P('win'), parts along dimension 0, may hold values from -0.375 to 0.375
- factor_three: float32 [384, 48], P(('win', 'wide')), parts along dimension 0, may hold values from -0.4375 to 0.4375
Outputs:
- basis_one: float32 [256, 48], P(('win', 'narrow')), parts along dimension 0
- basis_two: float32 [512, 48], P('win'), parts along dimension 0
- basis_three: float32 [384, 48], P(('win', 'wide')), parts along dimension 0
- core_unfolded: float32 [48, 4608], P(None, ('win', 'wide', 'narrow')), parts along dimension 1
There are 2 independent parts, one for each index of `win`. A program takes and returns all parts, laid end to end along the dimension named above; each array names one. Nothing has to cross between parts.
All inputs are finite; a program needn't handle non-finite values.
Results may differ from a plain program's by a relative error of at most 0.0003.
Values sent between devices are 32-bit elements; how exact they have to be, the bound alone decides.
No kernel may reach another device: no remote copies, remote signals or barrier semaphores. Data moves between devices by JAX's collectives and lax.ppermute only.
A program may use at most 64 MiB of HBM per device.

v0:
```python
import jax
import jax.numpy as jnp
from jax import lax
from jax.sharding import PartitionSpec as P

highest = lax.Precision.HIGHEST


def contract(form, left, right):
    return jnp.einsum(form, left, right, precision=highest)


def orthonormal(basis, gram):
    lower = jnp.linalg.cholesky(gram)
    return lax.linalg.triangular_solve(lower, basis, left_side=False, lower=True, transpose_a=True)


def full_core(partial_value):
    flat = partial_value.reshape(
        partial_value.shape[0], partial_value.shape[1] * partial_value.shape[2]
    )
    shares = lax.psum_scatter(flat, ("wide", "narrow"), scatter_dimension=1, tiled=True)
    whole = lax.all_gather(shares, ("wide", "narrow"), axis=1, tiled=True)
    return whole.reshape(partial_value.shape)


def on_device(window_data, factor_one, factor_two, factor_three):
    rank = factor_one.shape[1]
    along_two = contract("kij,jb->kib", window_data, factor_two)
    unfold_part = contract("kib,kc->ibc", along_two, factor_three).reshape(
        along_two.shape[1], rank * rank
    )
    unfold_rows = lax.psum_scatter(unfold_part, "wide", scatter_dimension=1, tiled=True)
    weights_one = lax.psum(jnp.dot(unfold_rows.T, factor_one, precision=highest), "narrow")
    product_one = lax.psum(jnp.dot(unfold_rows, weights_one, precision=highest), "wide")
    gram_one = lax.psum(jnp.dot(product_one.T, product_one, precision=highest), "narrow")
    basis_one = orthonormal(product_one, gram_one)
    along_one = contract("kij,ia->kaj", window_data, basis_one)
    core_two = full_core(
        contract("kab,kc->abc", contract("kaj,jb->kab", along_one, factor_two), factor_three)
    )
    spread_two = contract("abc,kc->kab", core_two, factor_three)
    product_two = lax.psum(contract("kaj,kab->jb", along_one, spread_two), ("wide", "narrow"))
    basis_two = orthonormal(product_two, jnp.dot(product_two.T, product_two, precision=highest))
    along_new = contract("kij,jb->kib", window_data, basis_two)
    unfold_three = contract("kib,ia->kab", along_new, basis_one)
    core_three = full_core(contract("kab,kc->abc", unfold_three, factor_three))
    product_three = lax.psum(contract("kab,abc->kc", unfold_three, core_three), "narrow")
    gram_three = lax.psum(jnp.dot(product_three.T, product_three, precision=highest), "wide")
    basis_three = orthonormal(product_three, gram_three)
    core_part = contract("kab,kc->abc", unfold_three, basis_three).reshape(rank, rank * rank)
    core_shares = lax.psum_scatter(core_part, ("wide", "narrow"), scatter_dimension=1, tiled=True)
    return (basis_one, basis_two, basis_three, core_shares)


def solution(mesh):
    return jax.shard_map(
        on_device,
        mesh=mesh,
        in_specs=(
            P(("win", "wide"), "narrow", None),
            P(("win", "narrow"), None),
            P("win", None),
            P(("win", "wide"), None),
        ),
        out_specs=(
            P(("win", "narrow"), None),
            P("win", None),
            P(("win", "wide"), None),
            P(None, ("win", "wide", "narrow")),
        ),
        check_vma=False,
    )
```

profile of v0, /device:TPU:0, one launch (start us, length us, event | category | flops | bytes accessed | tf_op | source)
XLA Modules:
  0.0 505.6 jit_solution(5925950153966513324)
XLA Ops:
  8.6 3.1 fusion.12
  13.9 67.9 %reduce-scatter.11.cloned.1.call-done = f32[64,288]{0,1:T(8,128)} async-done(((f32[64,2304]{0,1:T(8,128)}), f32[64,288]{0,1:T(8,128)}) %reduce-scatter.11.cloned.1.call-update) | async-done | bytes 73744 | tf_op jit(solution)/shard_map/reduce_scatter | solution.py:33
  83.1 3.5 psum.42
  87.7 34.9 %psum.43 = f32[64,48]{0,1:T(8,128)S(1)} all-reduce(f32[64,48]{0,1:T(8,128)S(1)} %fusion.35), channel_id=1, replica_groups=mesh['win'=2,'wide'=8,'narrow'=2] {'wide'}, use_global_device_ids=true, to_apply=%region_2.0 | all-reduce | flops 3072 | bytes 24576 | tf_op jit(solution)/shard_map/psum | solution.py:35
  122.8 3.4 psum.44
  126.3 4.4 cholesky.59
  132.0 3.7 custom-call.11
  138.7 3.1 fusion.31
  141.8 2.7 copy.45
  144.6 55.5 %reduce-scatter.13.cloned.1.call-done = f32[144,48]{1,0:T(8,128)} async-done(((f32[2304,48]{1,0:T(8,128)}), f32[144,48]{1,0:T(8,128)}) %reduce-scatter.13.cloned.1.call-update) | async-done | bytes 27664
  201.0 21.8 %all-gather = f32[16,144,48]{1,2,0:T(8,128)S(1)} all-gather(f32[1,144,48]{1,2,0:T(8,128)S(1)} %bitcast.116), channel_id=1, replica_groups=mesh['win'=2,'wide'=8,'narrow'=2] {'wide','narrow'}, dimensions={0}, use_global_device_ids=true | all-gather | bytes 470016 | tf_op jit(solution)/shard_map/all_gather | solution.py:23
  224.4 2.7 reshape.42
  227.2 4.7 convolution_bitcast_fusion.3
  233.1 57.9 %psum.45 = f32[256,48]{0,1:T(8,128)S(1)} all-reduce(f32[256,48]{0,1:T(8,128)S(1)} %convolution_bitcast_fusion.4), channel_id=1, replica_groups=mesh['win'=2,'wide'=8,'narrow'=2] {'wide','narrow'}, use_global_device_ids=true, to_apply=%region_7.0 | all-reduce | flops 12288 | bytes 98304 | tf_op jit(solution)/shard_map/psum | solution.py:43
  291.3 4.4 cholesky.70
  297.0 3.7 custom-call.12
  301.0 2.3 convolution_bitcast_fusion.2
  309.1 55.5 %reduce-scatter.15.cloned.1.call-done = f32[144,48]{1,0:T(8,128)} async-done(((f32[2304,48]{1,0:T(8,128)}), f32[144,48]{1,0:T(8,128)}) %reduce-scatter.15.cloned.1.call-update) | async-done | bytes 27664
  365.5 21.8 %all-gather.1 = f32[16,144,48]{1,2,0:T(8,128)S(1)} all-gather(f32[1,144,48]{1,2,0:T(8,128)S(1)} %bitcast.117), channel_id=1, replica_groups=mesh['win'=2,'wide'=8,'narrow'=2] {'wide','narrow'}, dimensions={0}, use_global_device_ids=true | all-gather | bytes 470016 | tf_op jit(solution)/shard_map/all_gather | solution.py:23
  391.9 3.5 psum.46
  395.6 33.0 %psum.47 = f32[48,48]{0,1:T(8,128)S(1)} all-reduce(f32[48,48]{0,1:T(8,128)S(1)} %fusion.38), channel_id=1, replica_groups=mesh['win'=2,'wide'=8,'narrow'=2] {'wide'}, use_global_device_ids=true, to_apply=%region_10.12 | all-reduce | flops 2304 | bytes 18432 | tf_op jit(solution)/shard_map/psum | solution.py:49
  428.7 4.4 cholesky.81
  434.4 3.7 custom-call.13
  441.9 55.6 %reduce-scatter.17.cloned.1.call-done = f32[144,48]{1,0:T(8,128)} async-done(((f32[2304,48]{1,0:T(8,128)}), f32[144,48]{1,0:T(8,128)}) %reduce-scatter.17.cloned.1.call-update) | async-done | bytes 27664
  (65 shorter events, 34.3 us)
Async XLA Ops:
  7.2 1.4 copy-start
  7.2 4.5 copy-start.3
  7.2 74.7 %reduce-scatter.11.cloned.1.call-start = ((), (), s32[]{:S(2)}) async-start(), calls=%async_computation.4 | async-start | bytes 1327104 | tf_op jit(solution)/shard_map/reduce_scatter | solution.py:33
  11.7 70.2 %copy-start.7 = (f32[64,48]{0,1:T(8,128)S(1)}, f32[64,48]{0,1:T(8,128)}, u32[]{:S(2)}) copy-start(f32[64,48]{0,1:T(8,128)} %param.6) | copy-start | bytes 36868
  13.9 186.2 %reduce-scatter.13.cloned.1.call-start = ((), (), s32[]{:S(2)}) async-start(), calls=%async_computation.5 | async-start | bytes 1253376
  135.9 1.1 copy-start.1
  136.0 1.1 copy-start.5
  144.5 220.0 %reduce-scatter.15.cloned.1.call-start = ((), (), s32[]{:S(2)}) async-start(), calls=%async_computation.6 | async-start | bytes 1253376
  297.0 6.3 %copy-start.2 = (f32[64,48]{0,1:T(8,128)S(1)}, f32[64,48]{0,1:T(8,128)}, u32[]{:S(2)}) copy-start(f32[64,48]{0,1:T(8,128)} %copy-done.1) | copy-start | bytes 36868
  301.0 4.5 copy-start.4
  309.0 188.4 %reduce-scatter.17.cloned.1.call-start = ((), (), s32[]{:S(2)}) async-start(), calls=%async_computation.7 | async-start | bytes 1253376
  438.3 3.6 copy-start.6
Sparse Core Ops, SparseCore 0:
  14.0 67.8 reduce-scatter.10
  144.7 55.3 reduce-scatter.12
  309.1 55.3 reduce-scatter.14
  442.0 55.4 reduce-scatter.16
where the time goes:
time: 506 us
  waiting for transfers between devices  235 us (46%)
  blocking collectives  180 us (36%)
  matrix products  30.3 us (6%)
  other arithmetic  28.2 us (6%)
  local copies, waits for them, and re-layouts  18.5 us (4%)
  between operations  14.1 us (3%)
    unnamed x7, waiting for transfers between devices  167 us
    reduce_scatter x1, waiting for transfers between devices, on_device(): lax.psum_scatter(unfold_part, 'wide', scatter_dimension=1, tiled=True)  67.9 us
    psum x1, blocking collectives, on_device(): lax.psum(contract('kaj,kab->jb', along_one, spread_two), ('wide', 'narrow'))  57.9 us
    all_gather x2, blocking collectives, full_core(): whole = lax.all_gather(shares, ('wide', 'narrow'), axis=1, tiled=True)  43.6 us
    psum x1, blocking collectives, on_device(): lax.psum(jnp.dot(unfold_rows, weights_one, precision=highest), 'wide')  34.9 us
    psum x1, blocking collectives, on_device(): lax.psum(jnp.dot(product_three.T, product_three, precision=highest), 'wide')  33 us
    dot_general x12, matrix products, contract(): return jnp.einsum(form, left, right, precision=highest)  26.7 us
    another operation x9, other arithmetic, orthonormal(): lower = jnp.linalg.cholesky(gram)  15.2 us
  transfers between devices with their start and end apart: 4, of which 4 were waited for; matrix products, arithmetic and copies ran while one was open for 0% of the time, Pallas kernels for 0%

commit v1 on v0

--- a/solution.py
+++ b/solution.py
@@ -20,7 +20,7 @@
         partial_value.shape[0], partial_value.shape[1] * partial_value.shape[2]
     )
     shares = lax.psum_scatter(flat, ("wide", "narrow"), scatter_dimension=1, tiled=True)
-    whole = lax.all_gather(shares, ("wide", "narrow"), axis=1, tiled=True)
+    whole = jnp.concatenate(lax.all_gather(shares, ("wide", "narrow")), axis=1)
     return whole.reshape(partial_value.shape)
 
 

time: 506 us -> 504 us (level)
    unnamed x24 -> x22, local copies, waits for them, and re-layouts: 12.9 us -> 10.6 us
where the time goes in v1:
time: 504 us; the launch traced here: 503 us
  waiting for transfers between devices  235 us (47%)
  blocking collectives  180 us (36%)
  matrix products  30.3 us (6%)
  other arithmetic  28.2 us (6%)
  local copies, waits for them, and re-layouts  15.9 us (3%)
  between operations  14.1 us (3%)
    unnamed x7, waiting for transfers between devices  167 us
    reduce_scatter x1, waiting for transfers between devices, on_device(): lax.psum_scatter(unfold_part, 'wide', scatter_dimension=1, tiled=True)  67.9 us
    psum x1, blocking collectives, on_device(): lax.psum(contract('kaj,kab->jb', along_one, spread_two), ('wide', 'narrow'))  57.9 us
    all_gather x2, blocking collectives, full_core(): whole = jnp.concatenate(lax.all_gather(shares, ('wide', 'narrow')), axis=1)  43.6 us
    psum x1, blocking collectives, on_device(): lax.psum(jnp.dot(unfold_rows, weights_one, precision=highest), 'wide')  34.9 us
    psum x1, blocking collectives, on_device(): lax.psum(jnp.dot(product_three.T, product_three, precision=highest), 'wide')  33 us
    dot_general x12, matrix products, contract(): return jnp.einsum(form, left, right, precision=highest)  26.7 us
    another operation x9, other arithmetic, orthonormal(): lower = jnp.linalg.cholesky(gram)  15.2 us
  transfers between devices with their start and end apart: 4, of which 4 were waited for; matrix products, arithmetic and copies ran while one was open for 0% of the time, Pallas kernels for 0%

profile of v1, /device:TPU:0, one launch (start us, length us, event | category | flops | bytes accessed | tf_op | source)
XLA Modules:
  0.0 503.0 jit_solution(2988590821013599557)
XLA Ops:
  8.6 3.1 fusion.12
  11.7 2.2 fusion.3
  13.9 67.9 %reduce-scatter.11.cloned.1.call-done = f32[64,288]{0,1:T(8,128)} async-done(((f32[64,2304]{0,1:T(8,128)}), f32[64,288]{0,1:T(8,128)}) %reduce-scatter.11.cloned.1.call-update) | async-done | bytes 73744 | tf_op jit(solution)/shard_map/reduce_scatter | solution.py:33
  83.1 3.5 psum.42
  87.7 34.9 %psum.43 = f32[64,48]{0,1:T(8,128)S(1)} all-reduce(f32[64,48]{0,1:T(8,128)S(1)} %fusion.35), channel_id=1, replica_groups=mesh['win'=2,'wide'=8,'narrow'=2] {'wide'}, use_global_device_ids=true, to_apply=%region_2.0 | all-reduce | flops 3072 | bytes 24576 | tf_op jit(solution)/shard_map/psum | solution.py:35
  122.8 3.4 psum.44
  126.3 4.4 cholesky.59
  132.0 3.7 custom-call.11
  138.7 3.1 fusion.31
  141.8 2.7 copy.60
  144.6 55.5 %reduce-scatter.13.cloned.1.call-done = f32[144,48]{1,0:T(8,128)} async-done(((f32[2304,48]{1,0:T(8,128)}), f32[144,48]{1,0:T(8,128)}) %reduce-scatter.13.cloned.1.call-update) | async-done | bytes 27664
  201.0 21.8 %all-gather = f32[768,144]{1,0:T(8,128)S(1)} all-gather(f32[48,144]{1,0:T(8,128)S(1)} %copy.55), channel_id=2, replica_groups=mesh['win'=2,'wide'=8,'narrow'=2] {'wide','narrow'}, dimensions={0}, use_global_device_ids=true | all-gather | bytes 470016 | tf_op jit(solution)/shard_map/all_gather | solution.py:23
  224.9 4.7 convolution_bitcast_fusion.3
  230.8 57.9 %psum.45 = f32[256,48]{0,1:T(8,128)S(1)} all-reduce(f32[256,48]{0,1:T(8,128)S(1)} %convolution_bitcast_fusion.4), channel_id=1, replica_groups=mesh['win'=2,'wide'=8,'narrow'=2] {'wide','narrow'}, use_global_device_ids=true, to_apply=%region_7.0 | all-reduce | flops 12288 | bytes 98304 | tf_op jit(solution)/shard_map/psum | solution.py:43
  289.0 4.4 cholesky.70
  294.7 3.7 custom-call.12
  298.6 2.3 convolution_bitcast_fusion.2
  306.7 55.5 %reduce-scatter.15.cloned.1.call-done = f32[144,48]{1,0:T(8,128)} async-done(((f32[2304,48]{1,0:T(8,128)}), f32[144,48]{1,0:T(8,128)}) %reduce-scatter.15.cloned.1.call-update) | async-done | bytes 27664
  363.3 21.8 %all-gather.1 = f32[768,144]{1,0:T(8,128)S(1)} all-gather(f32[48,144]{1,0:T(8,128)S(1)} %copy.57), channel_id=3, replica_groups=mesh['win'=2,'wide'=8,'narrow'=2] {'wide','narrow'}, dimensions={0}, use_global_device_ids=true | all-gather | bytes 470016 | tf_op jit(solution)/shard_map/all_gather | solution.py:23
  389.3 3.5 psum.46
  393.0 33.0 %psum.47 = f32[48,48]{0,1:T(8,128)S(1)} all-reduce(f32[48,48]{0,1:T(8,128)S(1)} %fusion.38), channel_id=1, replica_groups=mesh['win'=2,'wide'=8,'narrow'=2] {'wide'}, use_global_device_ids=true, to_apply=%region_10.12 | all-reduce | flops 2304 | bytes 18432 | tf_op jit(solution)/shard_map/psum | solution.py:49
  426.1 4.4 cholesky.81
  431.9 3.7 custom-call.13
  439.3 55.6 %reduce-scatter.17.cloned.1.call-done = f32[144,48]{1,0:T(8,128)} async-done(((f32[2304,48]{1,0:T(8,128)}), f32[144,48]{1,0:T(8,128)}) %reduce-scatter.17.cloned.1.call-update) | async-done | bytes 27664
  (63 shorter events, 32.2 us)
Async XLA Ops:
  7.2 1.4 copy-start
  7.2 4.5 copy-start.3
  7.2 74.7 %reduce-scatter.11.cloned.1.call-start = ((), (), s32[]{:S(2)}) async-start(), calls=%async_computation.4 | async-start | bytes 1327104 | tf_op jit(solution)/shard_map/reduce_scatter | solution.py:33
  11.7 70.2 %copy-start.7 = (f32[64,48]{0,1:T(8,128)S(1)}, f32[64,48]{0,1:T(8,128)}, u32[]{:S(2)}) copy-start(f32[64,48]{0,1:T(8,128)} %param.6) | copy-start | bytes 36868
  13.9 186.2 %reduce-scatter.13.cloned.1.call-start = ((), (), s32[]{:S(2)}) async-start(), calls=%async_computation.5 | async-start | bytes 1253376
  135.9 1.1 copy-start.1
  136.0 1.1 copy-start.5
  144.5 217.7 %reduce-scatter.15.cloned.1.call-start = ((), (), s32[]{:S(2)}) async-start(), calls=%async_computation.6 | async-start | bytes 1253376
  294.7 6.3 %copy-start.2 = (f32[64,48]{0,1:T(8,128)S(1)}, f32[64,48]{0,1:T(8,128)}, u32[]{:S(2)}) copy-start(f32[64,48]{0,1:T(8,128)} %copy-done.1) | copy-start | bytes 36868
  298.6 4.5 copy-start.4
  306.7 188.2 %reduce-scatter.17.cloned.1.call-start = ((), (), s32[]{:S(2)}) async-start(), calls=%async_computation.7 | async-start | bytes 1253376
  435.7 3.6 copy-start.6
Sparse Core Ops, SparseCore 0:
  14.0 67.8 reduce-scatter.10
  144.7 55.3 reduce-scatter.12
  306.8 55.4 reduce-scatter.14
  439.4 55.3 reduce-scatter.16
